TPU v7x, 512 devices: a whole 4x4x16 slice. The times are simulated.
512 devices in a mesh: row: 8 (over y, z_hi), col: 16 (over z_lo, core), depth: 4 (over x).
Axes of the slice: x: 4, y: 4, z: 16 (z_hi: 2, z_lo: 8; z = z_hi * 8 + z_lo), core: 2. Of those that a mesh axis runs over, the one named last changes fastest.
Arguments:
- a_tiles: bfloat16 [8, 16, 4, 4, 128, 128], P('row', 'col', 'depth'), may hold values from -0.625 to 0.625
- pair_lists: int32 [8, 16, 4, 16, 2, 4, 12], P('row', 'col', 'depth'), may hold values from 0 to 31, as said below
Outputs:
- product_blocks: float32 [8, 16, 12, 128, 128], P('row', 'col', 'depth')
Inputs may be any that keep to these rules, and one draw needn't show every extreme that they name: pair_lists[..., 0, m, o] is a left slot below 4, or 4 for an empty pair slot; the live pairs of a product block come first; pair_lists[..., 1, m, o] is a slot of the right panel.
All inputs are finite; a program needn't handle non-finite values.
Results may differ from a plain program's by a relative error of at most 0.0003.
Values may be sent and summed in bfloat16 or wider, within the bound.
A program may use at most 64 MiB of HBM per device.

v0:
```python
import jax
import jax.numpy as jnp
from jax import lax
from jax.sharding import PartitionSpec as P


def from_behind(block, axis, distance):
    devices = range(lax.axis_size(axis))
    route = [((i - distance) % len(devices), i) for i in devices]
    return lax.ppermute(block, axis, route)


def body(a_tiles, pair_lists):
    slot_count = a_tiles.shape[3]
    block_width = a_tiles.shape[4]
    own_tiles = a_tiles.reshape(slot_count, block_width, block_width)
    pair_table = pair_lists.reshape(pair_lists.shape[3:])
    shift_count = pair_table.shape[0]
    right_panel = lax.all_gather(own_tiles, "row", axis=0, tiled=True)
    zero_block = jnp.zeros((1, block_width, block_width), jnp.bfloat16)

    def contract(left_set, left_index, right_index):
        chosen = jnp.take(left_set, left_index, axis=0)
        partner = jnp.take(right_panel, right_index, axis=0)
        return jnp.einsum("moik,mojk->oij", chosen, partner, preferred_element_type=jnp.float32)

    def advance(step_index, carried):
        panel_tile, running = carried
        shifted = from_behind(panel_tile, "col", 1)
        padded = jnp.concatenate([shifted, zero_block], axis=0)
        return (
            shifted,
            running + contract(padded, pair_table[step_index, 0], pair_table[step_index, 1]),
        )

    opening = contract(
        jnp.concatenate([own_tiles, zero_block], axis=0), pair_table[0, 0], pair_table[0, 1]
    )
    carried = lax.fori_loop(1, shift_count, advance, (own_tiles, opening))
    running = carried[1]
    reduced = lax.psum_scatter(running, "depth", scatter_dimension=0, tiled=True)
    return reduced.reshape((1, 1) + reduced.shape)


def solution(mesh):
    placed = (
        P("row", "col", "depth", None, None, None),
        P("row", "col", "depth", None, None, None, None),
    )
    return jax.shard_map(
        body,
        mesh=mesh,
        in_specs=placed,
        out_specs=P("row", "col", "depth", None, None),
        check_vma=False,
    )
```

profile of v0, /device:TPU:8, one launch (start us, length us, event | category | flops | bytes accessed | tf_op | source)
XLA Modules:
  0.0 410.4 jit_solution(16223850005393163813)
XLA Ops:
  11.3 94.5 %all-gather.3.cloned.1.call-done = bf16[1,1,1,32,128,128]{5,4,2,1,0,3:T(8,128)(2,1)} async-done(((bf16[1,1,1,4,128,128]{5,4,2,1,0,3:T(8,128)(2,1)}), bf16[1,1,1,32,128,128]{5,4,2,1,0,3:T(8,128)(2,1)}) %all-gather.3.cloned.1.call-update) | async-done | bytes 1048592 | tf_op jit(solution)/shard_map/all_gather | solution.py:19
  105.8 3.2 gather_fusion.3
  109.0 3.1 fusion.10
  112.1 270.5 %while.17 = (s32[]{:T(128)}, bf16[4,128,128]{2,1,0:T(8,128)(2,1)S(1)}, f32[12,128,128]{2,1,0:T(8,128)}, s32[16,2,4,12]{3,2,1,0:T(4,128)S(1)}, bf16[32,128,128]{2...) while((s32[]{:T(128)}, bf16[4,128,128]{2,1,0:T(8,128)(2,1)S(1)}, ...), condition=%wide.region_1.0_spmd, body=%wide.region_0.3_spmd.sunk | while | flops 203098688 | bytes 12102445 | solution.py:39
  115.3 9.7 %collective-permute-done = bf16[4,128,128]{2,1,0:T(8,128)(2,1)S(1)} collective-permute-done((bf16[4,128,128]{2,1,0:T(8,128)(2,1)S(1)}, bf16[4,128,128]{2,1,0:T(8,128)(2,1)S(1)}, u32[]{:S(2)}, u32[]{:S(2)}) %collective-permute-start) | collective-permute-done | bytes 131104 | tf_op jit(solution)/shard_map/while/body/eval_jaxpr/ppermute | solution.py:10
  125.0 2.0 gather_fusion.1
  126.9 3.1 fusion.14
  130.1 1.9 collective-permute-start
  133.3 9.7 %collective-permute-done = bf16[4,128,128]{2,1,0:T(8,128)(2,1)S(1)} collective-permute-done((bf16[4,128,128]{2,1,0:T(8,128)(2,1)S(1)}, bf16[4,128,128]{2,1,0:T(8,128)(2,1)S(1)}, u32[]{:S(2)}, u32[]{:S(2)}) %collective-permute-start) | collective-permute-done | bytes 131104 | tf_op jit(solution)/shard_map/while/body/eval_jaxpr/ppermute | solution.py:10
  143.0 2.0 gather_fusion.1
  145.0 3.1 fusion.14
  148.1 1.9 collective-permute-start
  151.4 9.7 %collective-permute-done = bf16[4,128,128]{2,1,0:T(8,128)(2,1)S(1)} collective-permute-done((bf16[4,128,128]{2,1,0:T(8,128)(2,1)S(1)}, bf16[4,128,128]{2,1,0:T(8,128)(2,1)S(1)}, u32[]{:S(2)}, u32[]{:S(2)}) %collective-permute-start) | collective-permute-done | bytes 131104 | tf_op jit(solution)/shard_map/while/body/eval_jaxpr/ppermute | solution.py:10
  161.0 2.0 gather_fusion.1
  163.0 3.1 fusion.14
  166.2 1.9 collective-permute-start
  169.4 9.7 %collective-permute-done = bf16[4,128,128]{2,1,0:T(8,128)(2,1)S(1)} collective-permute-done((bf16[4,128,128]{2,1,0:T(8,128)(2,1)S(1)}, bf16[4,128,128]{2,1,0:T(8,128)(2,1)S(1)}, u32[]{:S(2)}, u32[]{:S(2)}) %collective-permute-start) | collective-permute-done | bytes 131104 | tf_op jit(solution)/shard_map/while/body/eval_jaxpr/ppermute | solution.py:10
  179.1 2.0 gather_fusion.1
  181.0 3.1 fusion.14
  184.2 1.9 collective-permute-start
  187.4 9.7 %collective-permute-done = bf16[4,128,128]{2,1,0:T(8,128)(2,1)S(1)} collective-permute-done((bf16[4,128,128]{2,1,0:T(8,128)(2,1)S(1)}, bf16[4,128,128]{2,1,0:T(8,128)(2,1)S(1)}, u32[]{:S(2)}, u32[]{:S(2)}) %collective-permute-start) | collective-permute-done | bytes 131104 | tf_op jit(solution)/shard_map/while/body/eval_jaxpr/ppermute | solution.py:10
  197.1 2.0 gather_fusion.1
  199.1 3.1 fusion.14
  202.2 1.9 collective-permute-start
  205.5 9.7 %collective-permute-done = bf16[4,128,128]{2,1,0:T(8,128)(2,1)S(1)} collective-permute-done((bf16[4,128,128]{2,1,0:T(8,128)(2,1)S(1)}, bf16[4,128,128]{2,1,0:T(8,128)(2,1)S(1)}, u32[]{:S(2)}, u32[]{:S(2)}) %collective-permute-start) | collective-permute-done | bytes 131104 | tf_op jit(solution)/shard_map/while/body/eval_jaxpr/ppermute | solution.py:10
  215.1 2.0 gather_fusion.1
  217.1 3.1 fusion.14
  220.3 1.9 collective-permute-start
  223.5 9.7 %collective-permute-done = bf16[4,128,128]{2,1,0:T(8,128)(2,1)S(1)} collective-permute-done((bf16[4,128,128]{2,1,0:T(8,128)(2,1)S(1)}, bf16[4,128,128]{2,1,0:T(8,128)(2,1)S(1)}, u32[]{:S(2)}, u32[]{:S(2)}) %collective-permute-start) | collective-permute-done | bytes 131104 | tf_op jit(solution)/shard_map/while/body/eval_jaxpr/ppermute | solution.py:10
  233.2 2.0 gather_fusion.1
  235.1 3.1 fusion.14
  238.3 1.9 collective-permute-start
  241.5 9.7 %collective-permute-done = bf16[4,128,128]{2,1,0:T(8,128)(2,1)S(1)} collective-permute-done((bf16[4,128,128]{2,1,0:T(8,128)(2,1)S(1)}, bf16[4,128,128]{2,1,0:T(8,128)(2,1)S(1)}, u32[]{:S(2)}, u32[]{:S(2)}) %collective-permute-start) | collective-permute-done | bytes 131104 | tf_op jit(solution)/shard_map/while/body/eval_jaxpr/ppermute | solution.py:10
  251.2 2.0 gather_fusion.1
  253.2 3.1 fusion.14
  256.3 1.9 collective-permute-start
  259.6 9.7 %collective-permute-done = bf16[4,128,128]{2,1,0:T(8,128)(2,1)S(1)} collective-permute-done((bf16[4,128,128]{2,1,0:T(8,128)(2,1)S(1)}, bf16[4,128,128]{2,1,0:T(8,128)(2,1)S(1)}, u32[]{:S(2)}, u32[]{:S(2)}) %collective-permute-start) | collective-permute-done | bytes 131104 | tf_op jit(solution)/shard_map/while/body/eval_jaxpr/ppermute | solution.py:10
  269.3 2.0 gather_fusion.1
  271.2 3.1 fusion.14
  274.4 1.9 collective-permute-start
  277.6 9.7 %collective-permute-done = bf16[4,128,128]{2,1,0:T(8,128)(2,1)S(1)} collective-permute-done((bf16[4,128,128]{2,1,0:T(8,128)(2,1)S(1)}, bf16[4,128,128]{2,1,0:T(8,128)(2,1)S(1)}, u32[]{:S(2)}, u32[]{:S(2)}) %collective-permute-start) | collective-permute-done | bytes 131104 | tf_op jit(solution)/shard_map/while/body/eval_jaxpr/ppermute | solution.py:10
  287.3 2.0 gather_fusion.1
  289.2 3.1 fusion.14
  292.4 1.9 collective-permute-start
  295.6 9.7 %collective-permute-done = bf16[4,128,128]{2,1,0:T(8,128)(2,1)S(1)} collective-permute-done((bf16[4,128,128]{2,1,0:T(8,128)(2,1)S(1)}, bf16[4,128,128]{2,1,0:T(8,128)(2,1)S(1)}, u32[]{:S(2)}, u32[]{:S(2)}) %collective-permute-start) | collective-permute-done | bytes 131104 | tf_op jit(solution)/shard_map/while/body/eval_jaxpr/ppermute | solution.py:10
  305.3 2.0 gather_fusion.1
  307.3 3.1 fusion.14
  310.5 1.9 collective-permute-start
  313.7 9.7 %collective-permute-done = bf16[4,128,128]{2,1,0:T(8,128)(2,1)S(1)} collective-permute-done((bf16[4,128,128]{2,1,0:T(8,128)(2,1)S(1)}, bf16[4,128,128]{2,1,0:T(8,128)(2,1)S(1)}, u32[]{:S(2)}, u32[]{:S(2)}) %collective-permute-start) | collective-permute-done | bytes 131104 | tf_op jit(solution)/shard_map/while/body/eval_jaxpr/ppermute | solution.py:10
  323.4 2.0 gather_fusion.1
  325.3 3.1 fusion.14
  328.5 1.9 collective-permute-start
  331.7 9.7 %collective-permute-done = bf16[4,128,128]{2,1,0:T(8,128)(2,1)S(1)} collective-permute-done((bf16[4,128,128]{2,1,0:T(8,128)(2,1)S(1)}, bf16[4,128,128]{2,1,0:T(8,128)(2,1)S(1)}, u32[]{:S(2)}, u32[]{:S(2)}) %collective-permute-start) | collective-permute-done | bytes 131104 | tf_op jit(solution)/shard_map/while/body/eval_jaxpr/ppermute | solution.py:10
  341.4 2.0 gather_fusion.1
  343.4 3.1 fusion.14
  346.5 1.9 collective-permute-start
  349.8 9.7 %collective-permute-done = bf16[4,128,128]{2,1,0:T(8,128)(2,1)S(1)} collective-permute-done((bf16[4,128,128]{2,1,0:T(8,128)(2,1)S(1)}, bf16[4,128,128]{2,1,0:T(8,128)(2,1)S(1)}, u32[]{:S(2)}, u32[]{:S(2)}) %collective-permute-start) | collective-permute-done | bytes 131104 | tf_op jit(solution)/shard_map/while/body/eval_jaxpr/ppermute | solution.py:10
  359.4 2.0 gather_fusion.1
  361.4 3.1 fusion.14
  364.6 1.9 collective-permute-start
  367.8 9.7 %collective-permute-done = bf16[4,128,128]{2,1,0:T(8,128)(2,1)S(1)} collective-permute-done((bf16[4,128,128]{2,1,0:T(8,128)(2,1)S(1)}, bf16[4,128,128]{2,1,0:T(8,128)(2,1)S(1)}, u32[]{:S(2)}, u32[]{:S(2)}) %collective-permute-start) | collective-permute-done | bytes 131104 | tf_op jit(solution)/shard_map/while/body/eval_jaxpr/ppermute | solution.py:10
  377.5 2.0 gather_fusion.1
  379.4 3.1 fusion.14
  382.6 21.0 %reduce-scatter.2.cloned.1.call-done = f32[3,128,128]{2,1,0:T(8,128)} async-done(((f32[12,128,128]{2,1,0:T(8,128)}), f32[3,128,128]{2,1,0:T(8,128)}) %reduce-scatter.2.cloned.1.call-update) | async-done | bytes 196624 | tf_op jit(solution)/shard_map/reduce_scatter | solution.py:41
  (171 shorter events, 26.0 us)
Async XLA Ops:
  6.5 99.3 %all-gather.3.cloned.1.call-start = ((), (), s32[]{:S(2)}) async-start(), calls=%async_computation.2 | async-start | bytes 1179648 | tf_op jit(solution)/shard_map/all_gather | solution.py:19
  8.1 395.5 %reduce-scatter.2.cloned.1.call-start = ((), (), s32[]{:S(2)}) async-start(), calls=%async_computation.1 | async-start | bytes 983040 | tf_op jit(solution)/shard_map/reduce_scatter | solution.py:41
  109.0 3.1 copy-start
  109.0 3.1 copy-start.1
  112.1 12.9 %collective-permute-start = (bf16[4,128,128]{2,1,0:T(8,128)(2,1)S(1)}, bf16[4,128,128]{2,1,0:T(8,128)(2,1)S(1)}, u32[]{:S(2)}, u32[]{:S(2)}) collective-permute-start(bf16[4,128,128]{2,1,0:T(8,128)(2,1)S(1)} %get-tuple-element.209), channel_id=1, source_target_pairs={{60,0},{0,4},{4,8},{8,12},{12,16},{16,20},{20,24},{24,28},{28,32},... | collective-permute-start | bytes 393224 | tf_op jit(solution)/shard_map/while/body/eval_jaxpr/ppermute | solution.py:10
  130.1 12.9 %collective-permute-start = (bf16[4,128,128]{2,1,0:T(8,128)(2,1)S(1)}, bf16[4,128,128]{2,1,0:T(8,128)(2,1)S(1)}, u32[]{:S(2)}, u32[]{:S(2)}) collective-permute-start(bf16[4,128,128]{2,1,0:T(8,128)(2,1)S(1)} %get-tuple-element.209), channel_id=1, source_target_pairs={{60,0},{0,4},{4,8},{8,12},{12,16},{16,20},{20,24},{24,28},{28,32},... | collective-permute-start | bytes 393224 | tf_op jit(solution)/shard_map/while/body/eval_jaxpr/ppermute | solution.py:10
  148.1 12.9 %collective-permute-start = (bf16[4,128,128]{2,1,0:T(8,128)(2,1)S(1)}, bf16[4,128,128]{2,1,0:T(8,128)(2,1)S(1)}, u32[]{:S(2)}, u32[]{:S(2)}) collective-permute-start(bf16[4,128,128]{2,1,0:T(8,128)(2,1)S(1)} %get-tuple-element.209), channel_id=1, source_target_pairs={{60,0},{0,4},{4,8},{8,12},{12,16},{16,20},{20,24},{24,28},{28,32},... | collective-permute-start | bytes 393224 | tf_op jit(solution)/shard_map/while/body/eval_jaxpr/ppermute | solution.py:10
  166.2 12.9 %collective-permute-start = (bf16[4,128,128]{2,1,0:T(8,128)(2,1)S(1)}, bf16[4,128,128]{2,1,0:T(8,128)(2,1)S(1)}, u32[]{:S(2)}, u32[]{:S(2)}) collective-permute-start(bf16[4,128,128]{2,1,0:T(8,128)(2,1)S(1)} %get-tuple-element.209), channel_id=1, source_target_pairs={{60,0},{0,4},{4,8},{8,12},{12,16},{16,20},{20,24},{24,28},{28,32},... | collective-permute-start | bytes 393224 | tf_op jit(solution)/shard_map/while/body/eval_jaxpr/ppermute | solution.py:10
  184.2 12.9 %collective-permute-start = (bf16[4,128,128]{2,1,0:T(8,128)(2,1)S(1)}, bf16[4,128,128]{2,1,0:T(8,128)(2,1)S(1)}, u32[]{:S(2)}, u32[]{:S(2)}) collective-permute-start(bf16[4,128,128]{2,1,0:T(8,128)(2,1)S(1)} %get-tuple-element.209), channel_id=1, source_target_pairs={{60,0},{0,4},{4,8},{8,12},{12,16},{16,20},{20,24},{24,28},{28,32},... | collective-permute-start | bytes 393224 | tf_op jit(solution)/shard_map/while/body/eval_jaxpr/ppermute | solution.py:10
  202.2 12.9 %collective-permute-start = (bf16[4,128,128]{2,1,0:T(8,128)(2,1)S(1)}, bf16[4,128,128]{2,1,0:T(8,128)(2,1)S(1)}, u32[]{:S(2)}, u32[]{:S(2)}) collective-permute-start(bf16[4,128,128]{2,1,0:T(8,128)(2,1)S(1)} %get-tuple-element.209), channel_id=1, source_target_pairs={{60,0},{0,4},{4,8},{8,12},{12,16},{16,20},{20,24},{24,28},{28,32},... | collective-permute-start | bytes 393224 | tf_op jit(solution)/shard_map/while/body/eval_jaxpr/ppermute | solution.py:10
  220.3 12.9 %collective-permute-start = (bf16[4,128,128]{2,1,0:T(8,128)(2,1)S(1)}, bf16[4,128,128]{2,1,0:T(8,128)(2,1)S(1)}, u32[]{:S(2)}, u32[]{:S(2)}) collective-permute-start(bf16[4,128,128]{2,1,0:T(8,128)(2,1)S(1)} %get-tuple-element.209), channel_id=1, source_target_pairs={{60,0},{0,4},{4,8},{8,12},{12,16},{16,20},{20,24},{24,28},{28,32},... | collective-permute-start | bytes 393224 | tf_op jit(solution)/shard_map/while/body/eval_jaxpr/ppermute | solution.py:10
  238.3 12.9 %collective-permute-start = (bf16[4,128,128]{2,1,0:T(8,128)(2,1)S(1)}, bf16[4,128,128]{2,1,0:T(8,128)(2,1)S(1)}, u32[]{:S(2)}, u32[]{:S(2)}) collective-permute-start(bf16[4,128,128]{2,1,0:T(8,128)(2,1)S(1)} %get-tuple-element.209), channel_id=1, source_target_pairs={{60,0},{0,4},{4,8},{8,12},{12,16},{16,20},{20,24},{24,28},{28,32},... | collective-permute-start | bytes 393224 | tf_op jit(solution)/shard_map/while/body/eval_jaxpr/ppermute | solution.py:10
  256.3 12.9 %collective-permute-start = (bf16[4,128,128]{2,1,0:T(8,128)(2,1)S(1)}, bf16[4,128,128]{2,1,0:T(8,128)(2,1)S(1)}, u32[]{:S(2)}, u32[]{:S(2)}) collective-permute-start(bf16[4,128,128]{2,1,0:T(8,128)(2,1)S(1)} %get-tuple-element.209), channel_id=1, source_target_pairs={{60,0},{0,4},{4,8},{8,12},{12,16},{16,20},{20,24},{24,28},{28,32},... | collective-permute-start | bytes 393224 | tf_op jit(solution)/shard_map/while/body/eval_jaxpr/ppermute | solution.py:10
  274.4 12.9 %collective-permute-start = (bf16[4,128,128]{2,1,0:T(8,128)(2,1)S(1)}, bf16[4,128,128]{2,1,0:T(8,128)(2,1)S(1)}, u32[]{:S(2)}, u32[]{:S(2)}) collective-permute-start(bf16[4,128,128]{2,1,0:T(8,128)(2,1)S(1)} %get-tuple-element.209), channel_id=1, source_target_pairs={{60,0},{0,4},{4,8},{8,12},{12,16},{16,20},{20,24},{24,28},{28,32},... | collective-permute-start | bytes 393224 | tf_op jit(solution)/shard_map/while/body/eval_jaxpr/ppermute | solution.py:10
  292.4 12.9 %collective-permute-start = (bf16[4,128,128]{2,1,0:T(8,128)(2,1)S(1)}, bf16[4,128,128]{2,1,0:T(8,128)(2,1)S(1)}, u32[]{:S(2)}, u32[]{:S(2)}) collective-permute-start(bf16[4,128,128]{2,1,0:T(8,128)(2,1)S(1)} %get-tuple-element.209), channel_id=1, source_target_pairs={{60,0},{0,4},{4,8},{8,12},{12,16},{16,20},{20,24},{24,28},{28,32},... | collective-permute-start | bytes 393224 | tf_op jit(solution)/shard_map/while/body/eval_jaxpr/ppermute | solution.py:10
  310.5 12.9 %collective-permute-start = (bf16[4,128,128]{2,1,0:T(8,128)(2,1)S(1)}, bf16[4,128,128]{2,1,0:T(8,128)(2,1)S(1)}, u32[]{:S(2)}, u32[]{:S(2)}) collective-permute-start(bf16[4,128,128]{2,1,0:T(8,128)(2,1)S(1)} %get-tuple-element.209), channel_id=1, source_target_pairs={{60,0},{0,4},{4,8},{8,12},{12,16},{16,20},{20,24},{24,28},{28,32},... | collective-permute-start | bytes 393224 | tf_op jit(solution)/shard_map/while/body/eval_jaxpr/ppermute | solution.py:10
  328.5 12.9 %collective-permute-start = (bf16[4,128,128]{2,1,0:T(8,128)(2,1)S(1)}, bf16[4,128,128]{2,1,0:T(8,128)(2,1)S(1)}, u32[]{:S(2)}, u32[]{:S(2)}) collective-permute-start(bf16[4,128,128]{2,1,0:T(8,128)(2,1)S(1)} %get-tuple-element.209), channel_id=1, source_target_pairs={{60,0},{0,4},{4,8},{8,12},{12,16},{16,20},{20,24},{24,28},{28,32},... | collective-permute-start | bytes 393224 | tf_op jit(solution)/shard_map/while/body/eval_jaxpr/ppermute | solution.py:10
  346.5 12.9 %collective-permute-start = (bf16[4,128,128]{2,1,0:T(8,128)(2,1)S(1)}, bf16[4,128,128]{2,1,0:T(8,128)(2,1)S(1)}, u32[]{:S(2)}, u32[]{:S(2)}) collective-permute-start(bf16[4,128,128]{2,1,0:T(8,128)(2,1)S(1)} %get-tuple-element.209), channel_id=1, source_target_pairs={{60,0},{0,4},{4,8},{8,12},{12,16},{16,20},{20,24},{24,28},{28,32},... | collective-permute-start | bytes 393224 | tf_op jit(solution)/shard_map/while/body/eval_jaxpr/ppermute | solution.py:10
  364.6 12.9 %collective-permute-start = (bf16[4,128,128]{2,1,0:T(8,128)(2,1)S(1)}, bf16[4,128,128]{2,1,0:T(8,128)(2,1)S(1)}, u32[]{:S(2)}, u32[]{:S(2)}) collective-permute-start(bf16[4,128,128]{2,1,0:T(8,128)(2,1)S(1)} %get-tuple-element.209), channel_id=1, source_target_pairs={{60,0},{0,4},{4,8},{8,12},{12,16},{16,20},{20,24},{24,28},{28,32},... | collective-permute-start | bytes 393224 | tf_op jit(solution)/shard_map/while/body/eval_jaxpr/ppermute | solution.py:10
Sparse Core Ops, SparseCore 0:
  10.6 95.2 all-gather.2
  382.7 20.7 reduce-scatter.1
where the time goes:
time: 412 us; the launch traced here: 410 us
  waiting for transfers between devices  261 us (63%)
  local copies, waits for them, and re-layouts  56 us (14%)
  matrix products  50.3 us (12%)
  starting transfers between devices  28.8 us (7%)
  between operations  13.4 us (3%)
    ppermute x15, waiting for transfers between devices, from_behind(): return lax.ppermute(block, axis, route)  145 us
    all_gather x1, waiting for transfers between devices, body(): right_panel = lax.all_gather(own_tiles, 'row', axis=0, tiled=True)  94.5 us
    dot_general x16, matrix products, contract(): jnp.einsum('moik,mojk->oij', chosen, partner, preferred_element_type=jnp....  50.3 us
    gather x16, local copies, waits for them, and re-layouts, contract(): chosen = jnp.take(left_set, left_index, axis=0)  30.1 us
    ppermute x15, starting transfers between devices, from_behind(): return lax.ppermute(block, axis, route)  28.8 us
    reduce_scatter x1, waiting for transfers between devices, body(): lax.psum_scatter(running, 'depth', scatter_dimension=0, tiled=True)  21 us
    gather x16, local copies, waits for them, and re-layouts, contract(): partner = jnp.take(right_panel, right_index, axis=0)  15.9 us
  transfers between devices with their start and end apart: 17, of which 17 were waited for; matrix products, arithmetic and copies ran while one was open for 5% of the time, Pallas kernels for 0%

commit v1 on v0

--- a/solution.py
+++ b/solution.py
@@ -16,7 +16,10 @@
     own_tiles = a_tiles.reshape(slot_count, block_width, block_width)
     pair_table = pair_lists.reshape(pair_lists.shape[3:])
     shift_count = pair_table.shape[0]
-    right_panel = lax.all_gather(own_tiles, "row", axis=0, tiled=True)
+    size = lax.axis_size("row")
+    blocks = jnp.stack([own_tiles for _ in range(size)])
+    blocks = lax.all_to_all(blocks, "row", split_axis=0, concat_axis=0)
+    right_panel = jnp.concatenate(blocks, axis=0)
     zero_block = jnp.zeros((1, block_width, block_width), jnp.bfloat16)
 
     def contract(left_set, left_index, right_index):

time: 412 us -> 371 us (0.900)
  waiting for transfers between devices: 261 us -> 195 us
  starting transfers between devices: 28.8 us -> 56.7 us
    all_gather x1 -> x0, waiting for transfers between devices: 94.5 us -> none  [body(): right_panel = lax.all_gather(own_tiles, 'row', axis=0, tiled=True)]
    all_to_all x0 -> x1, waiting for transfers between devices: none -> 25.2 us  [body(): blocks = lax.all_to_all(blocks, 'row', split_axis=0, concat_axis=0)]
    all_to_all x0 -> x1, starting transfers between devices: none -> 18.2 us  [body(): blocks = lax.all_to_all(blocks, 'row', split_axis=0, concat_axis=0)]
    ppermute x15, starting transfers between devices: 28.8 us -> 38.5 us  [from_behind(): return lax.ppermute(block, axis, route)]
  transfers between devices with their start and end apart: 17 -> 17, of which waited for: 17 -> 17; matrix products, arithmetic and copies ran while one was open for 5% -> 6% of each run, Pallas kernels for 0% -> 0%
where the time goes in v1:
time: 371 us; the launch traced here: 370 us
  waiting for transfers between devices  195 us (53%)
  starting transfers between devices  56.7 us (15%)
  local copies, waits for them, and re-layouts  53.6 us (14%)
  matrix products  50.1 us (14%)
  between operations  13.4 us (4%)
    ppermute x15, waiting for transfers between devices, from_behind(): return lax.ppermute(block, axis, route)  148 us
    dot_general x16, matrix products, contract(): jnp.einsum('moik,mojk->oij', chosen, partner, preferred_element_type=jnp....  50.1 us
    ppermute x15, starting transfers between devices, from_behind(): return lax.ppermute(block, axis, route)  38.5 us
    gather x16, local copies, waits for them, and re-layouts, contract(): chosen = jnp.take(left_set, left_index, axis=0)  30.1 us
    all_to_all x1, waiting for transfers between devices, body(): blocks = lax.all_to_all(blocks, 'row', split_axis=0, concat_axis=0)  25.2 us
    reduce_scatter x1, waiting for transfers between devices, body(): lax.psum_scatter(running, 'depth', scatter_dimension=0, tiled=True)  21.4 us
    all_to_all x1, starting transfers between devices, body(): blocks = lax.all_to_all(blocks, 'row', split_axis=0, concat_axis=0)  18.2 us
    gather x16, local copies, waits for them, and re-layouts, contract(): partner = jnp.take(right_panel, right_index, axis=0)  14.7 us
  transfers between devices with their start and end apart: 17, of which 17 were waited for; matrix products, arithmetic and copies ran while one was open for 6% of the time, Pallas kernels for 0%

profile of v1, /device:TPU:8, one launch (start us, length us, event | category | flops | bytes accessed | tf_op | source)
XLA Modules:
  0.0 369.9 jit_solution(18383140428410427107)
XLA Ops:
  8.6 18.2 %all-to-all-start = ((bf16[8,4,128,128]{3,2,1,0:T(8,128)(2,1)}), bf16[8,4,128,128]{3,2,1,0:T(8,128)(2,1)S(1)}, u32[]{:S(2)}, u32[]{:S(2)}) async-start(bf16[8,4,128,128]{3,2,1,0:T(8,128)(2,1)} %stack.3), calls=%async_computation | async-start | bytes 2097152 | tf_op jit(solution)/shard_map/all_to_all | solution.py:21
  28.3 25.2 %all-to-all-done = bf16[8,4,128,128]{3,2,1,0:T(8,128)(2,1)S(1)} async-done(((bf16[8,4,128,128]{3,2,1,0:T(8,128)(2,1)}), bf16[8,4,128,128]{3,2,1,0:T(8,128)(2,1)S(1)}, u32[]{:S(2)}, u32[]{:S(2)}) %all-to-all-start) | async-done | bytes 1048608 | tf_op jit(solution)/shard_map/all_to_all | solution.py:21
  53.4 1.9 gather_fusion.3
  55.4 3.0 fusion.10
  58.3 283.3 %while.17 = (s32[]{:T(128)}, bf16[4,128,128]{2,1,0:T(8,128)(2,1)S(1)}, f32[12,128,128]{2,1,0:T(8,128)}, s32[16,2,4,12]{3,2,1,0:T(4,128)S(1)}, bf16[32,128,128]{2...) while((s32[]{:T(128)}, bf16[4,128,128]{2,1,0:T(8,128)(2,1)S(1)}, ...), condition=%wide.region_1.0_spmd, body=%wide.region_0.3_spmd.sunk | while | flops 203098688 | bytes 12102445 | solution.py:42
  61.6 22.6 %collective-permute-done = bf16[4,128,128]{2,1,0:T(8,128)(2,1)S(1)} collective-permute-done((bf16[4,128,128]{2,1,0:T(8,128)(2,1)S(1)}, bf16[4,128,128]{2,1,0:T(8,128)(2,1)S(1)}, u32[]{:S(2)}, u32[]{:S(2)}) %collective-permute-start) | collective-permute-done | bytes 131104 | tf_op jit(solution)/shard_map/while/body/eval_jaxpr/ppermute | solution.py:10
  84.2 1.9 gather_fusion.1
  86.1 3.1 fusion.14
  89.3 10.1 %collective-permute-start = (bf16[4,128,128]{2,1,0:T(8,128)(2,1)S(1)}, bf16[4,128,128]{2,1,0:T(8,128)(2,1)S(1)}, u32[]{:S(2)}, u32[]{:S(2)}) collective-permute-start(bf16[4,128,128]{2,1,0:T(8,128)(2,1)S(1)} %get-tuple-element.209), channel_id=1, source_target_pairs={{60,0},{0,4},{4,8},{8,12},{12,16},{16,20},{20,24},{24,28},{28,32},... | collective-permute-start | bytes 393224 | tf_op jit(solution)/shard_map/while/body/eval_jaxpr/ppermute | solution.py:10
  102.2 1.9 gather_fusion.1
  104.2 3.1 fusion.14
  107.3 3.5 collective-permute-start
  112.1 8.1 %collective-permute-done = bf16[4,128,128]{2,1,0:T(8,128)(2,1)S(1)} collective-permute-done((bf16[4,128,128]{2,1,0:T(8,128)(2,1)S(1)}, bf16[4,128,128]{2,1,0:T(8,128)(2,1)S(1)}, u32[]{:S(2)}, u32[]{:S(2)}) %collective-permute-start) | collective-permute-done | bytes 131104 | tf_op jit(solution)/shard_map/while/body/eval_jaxpr/ppermute | solution.py:10
  120.2 1.9 gather_fusion.1
  122.2 3.1 fusion.14
  125.3 1.9 collective-permute-start
  128.6 9.7 %collective-permute-done = bf16[4,128,128]{2,1,0:T(8,128)(2,1)S(1)} collective-permute-done((bf16[4,128,128]{2,1,0:T(8,128)(2,1)S(1)}, bf16[4,128,128]{2,1,0:T(8,128)(2,1)S(1)}, u32[]{:S(2)}, u32[]{:S(2)}) %collective-permute-start) | collective-permute-done | bytes 131104 | tf_op jit(solution)/shard_map/while/body/eval_jaxpr/ppermute | solution.py:10
  138.3 1.9 gather_fusion.1
  140.2 3.1 fusion.14
  143.4 1.9 collective-permute-start
  146.6 9.7 %collective-permute-done = bf16[4,128,128]{2,1,0:T(8,128)(2,1)S(1)} collective-permute-done((bf16[4,128,128]{2,1,0:T(8,128)(2,1)S(1)}, bf16[4,128,128]{2,1,0:T(8,128)(2,1)S(1)}, u32[]{:S(2)}, u32[]{:S(2)}) %collective-permute-start) | collective-permute-done | bytes 131104 | tf_op jit(solution)/shard_map/while/body/eval_jaxpr/ppermute | solution.py:10
  156.3 1.9 gather_fusion.1
  158.2 3.1 fusion.14
  161.4 1.9 collective-permute-start
  164.6 9.7 %collective-permute-done = bf16[4,128,128]{2,1,0:T(8,128)(2,1)S(1)} collective-permute-done((bf16[4,128,128]{2,1,0:T(8,128)(2,1)S(1)}, bf16[4,128,128]{2,1,0:T(8,128)(2,1)S(1)}, u32[]{:S(2)}, u32[]{:S(2)}) %collective-permute-start) | collective-permute-done | bytes 131104 | tf_op jit(solution)/shard_map/while/body/eval_jaxpr/ppermute | solution.py:10
  174.3 1.9 gather_fusion.1
  176.2 3.1 fusion.14
  179.4 1.9 collective-permute-start
  182.6 9.7 %collective-permute-done = bf16[4,128,128]{2,1,0:T(8,128)(2,1)S(1)} collective-permute-done((bf16[4,128,128]{2,1,0:T(8,128)(2,1)S(1)}, bf16[4,128,128]{2,1,0:T(8,128)(2,1)S(1)}, u32[]{:S(2)}, u32[]{:S(2)}) %collective-permute-start) | collective-permute-done | bytes 131104 | tf_op jit(solution)/shard_map/while/body/eval_jaxpr/ppermute | solution.py:10
  192.3 1.9 gather_fusion.1
  194.3 3.1 fusion.14
  197.4 1.9 collective-permute-start
  200.7 9.7 %collective-permute-done = bf16[4,128,128]{2,1,0:T(8,128)(2,1)S(1)} collective-permute-done((bf16[4,128,128]{2,1,0:T(8,128)(2,1)S(1)}, bf16[4,128,128]{2,1,0:T(8,128)(2,1)S(1)}, u32[]{:S(2)}, u32[]{:S(2)}) %collective-permute-start) | collective-permute-done | bytes 131104 | tf_op jit(solution)/shard_map/while/body/eval_jaxpr/ppermute | solution.py:10
  210.3 1.9 gather_fusion.1
  212.3 3.1 fusion.14
  215.5 1.9 collective-permute-start
  218.7 9.7 %collective-permute-done = bf16[4,128,128]{2,1,0:T(8,128)(2,1)S(1)} collective-permute-done((bf16[4,128,128]{2,1,0:T(8,128)(2,1)S(1)}, bf16[4,128,128]{2,1,0:T(8,128)(2,1)S(1)}, u32[]{:S(2)}, u32[]{:S(2)}) %collective-permute-start) | collective-permute-done | bytes 131104 | tf_op jit(solution)/shard_map/while/body/eval_jaxpr/ppermute | solution.py:10
  228.4 1.9 gather_fusion.1
  230.3 3.1 fusion.14
  233.5 1.9 collective-permute-start
  236.7 9.7 %collective-permute-done = bf16[4,128,128]{2,1,0:T(8,128)(2,1)S(1)} collective-permute-done((bf16[4,128,128]{2,1,0:T(8,128)(2,1)S(1)}, bf16[4,128,128]{2,1,0:T(8,128)(2,1)S(1)}, u32[]{:S(2)}, u32[]{:S(2)}) %collective-permute-start) | collective-permute-done | bytes 131104 | tf_op jit(solution)/shard_map/while/body/eval_jaxpr/ppermute | solution.py:10
  246.4 1.9 gather_fusion.1
  248.3 3.1 fusion.14
  251.5 1.9 collective-permute-start
  254.7 9.7 %collective-permute-done = bf16[4,128,128]{2,1,0:T(8,128)(2,1)S(1)} collective-permute-done((bf16[4,128,128]{2,1,0:T(8,128)(2,1)S(1)}, bf16[4,128,128]{2,1,0:T(8,128)(2,1)S(1)}, u32[]{:S(2)}, u32[]{:S(2)}) %collective-permute-start) | collective-permute-done | bytes 131104 | tf_op jit(solution)/shard_map/while/body/eval_jaxpr/ppermute | solution.py:10
  264.4 1.9 gather_fusion.1
  266.4 3.1 fusion.14
  269.5 1.9 collective-permute-start
  272.8 9.7 %collective-permute-done = bf16[4,128,128]{2,1,0:T(8,128)(2,1)S(1)} collective-permute-done((bf16[4,128,128]{2,1,0:T(8,128)(2,1)S(1)}, bf16[4,128,128]{2,1,0:T(8,128)(2,1)S(1)}, u32[]{:S(2)}, u32[]{:S(2)}) %collective-permute-start) | collective-permute-done | bytes 131104 | tf_op jit(solution)/shard_map/while/body/eval_jaxpr/ppermute | solution.py:10
  282.4 1.9 gather_fusion.1
  284.4 3.1 fusion.14
  287.6 1.9 collective-permute-start
  290.8 9.7 %collective-permute-done = bf16[4,128,128]{2,1,0:T(8,128)(2,1)S(1)} collective-permute-done((bf16[4,128,128]{2,1,0:T(8,128)(2,1)S(1)}, bf16[4,128,128]{2,1,0:T(8,128)(2,1)S(1)}, u32[]{:S(2)}, u32[]{:S(2)}) %collective-permute-start) | collective-permute-done | bytes 131104 | tf_op jit(solution)/shard_map/while/body/eval_jaxpr/ppermute | solution.py:10
  300.5 1.9 gather_fusion.1
  302.4 3.1 fusion.14
  305.6 1.9 collective-permute-start
  308.8 9.7 %collective-permute-done = bf16[4,128,128]{2,1,0:T(8,128)(2,1)S(1)} collective-permute-done((bf16[4,128,128]{2,1,0:T(8,128)(2,1)S(1)}, bf16[4,128,128]{2,1,0:T(8,128)(2,1)S(1)}, u32[]{:S(2)}, u32[]{:S(2)}) %collective-permute-start) | collective-permute-done | bytes 131104 | tf_op jit(solution)/shard_map/while/body/eval_jaxpr/ppermute | solution.py:10
  318.5 1.9 gather_fusion.1
  320.4 3.1 fusion.14
  323.6 1.9 collective-permute-start
  326.8 9.7 %collective-permute-done = bf16[4,128,128]{2,1,0:T(8,128)(2,1)S(1)} collective-permute-done((bf16[4,128,128]{2,1,0:T(8,128)(2,1)S(1)}, bf16[4,128,128]{2,1,0:T(8,128)(2,1)S(1)}, u32[]{:S(2)}, u32[]{:S(2)}) %collective-permute-start) | collective-permute-done | bytes 131104 | tf_op jit(solution)/shard_map/while/body/eval_jaxpr/ppermute | solution.py:10
  336.5 1.9 gather_fusion.1
  338.5 3.1 fusion.14
  341.7 21.4 %reduce-scatter.2.cloned.1.call-done = f32[3,128,128]{2,1,0:T(8,128)} async-done(((f32[12,128,128]{2,1,0:T(8,128)}), f32[3,128,128]{2,1,0:T(8,128)}) %reduce-scatter.2.cloned.1.call-update) | async-done | bytes 196624 | tf_op jit(solution)/shard_map/reduce_scatter | solution.py:44
  (169 shorter events, 26.3 us)
Async XLA Ops:
  7.4 19.4 %copy-start = (s32[1,1,1,16,2,4,12]{3,5,6,4,2,1,0:T(4,128)S(1)}, s32[1,1,1,16,2,4,12]{3,5,6,4,2,1,0:T(4,128)}, u32[]{:S(2)}) copy-start(s32[1,1,1,16,2,4,12]{3,5,6,4,2,1,0:T(4,128)} %param.9) | copy-start | bytes 18436
  8.6 44.8 %all-to-all-start = ((bf16[8,4,128,128]{3,2,1,0:T(8,128)(2,1)}), bf16[8,4,128,128]{3,2,1,0:T(8,128)(2,1)S(1)}, u32[]{:S(2)}, u32[]{:S(2)}) async-start(bf16[8,4,128,128]{3,2,1,0:T(8,128)(2,1)} %stack.3), calls=%async_computation | async-start | bytes 2097152 | tf_op jit(solution)/shard_map/all_to_all | solution.py:21
  26.8 336.2 %reduce-scatter.2.cloned.1.call-start = ((), (), s32[]{:S(2)}) async-start(), calls=%async_computation.2 | async-start | bytes 983040 | tf_op jit(solution)/shard_map/reduce_scatter | solution.py:44
  58.3 25.8 %collective-permute-start = (bf16[4,128,128]{2,1,0:T(8,128)(2,1)S(1)}, bf16[4,128,128]{2,1,0:T(8,128)(2,1)S(1)}, u32[]{:S(2)}, u32[]{:S(2)}) collective-permute-start(bf16[4,128,128]{2,1,0:T(8,128)(2,1)S(1)} %get-tuple-element.209), channel_id=1, source_target_pairs={{60,0},{0,4},{4,8},{8,12},{12,16},{16,20},{20,24},{24,28},{28,32},... | collective-permute-start | bytes 393224 | tf_op jit(solution)/shard_map/while/body/eval_jaxpr/ppermute | solution.py:10
  89.3 12.9 %collective-permute-start = (bf16[4,128,128]{2,1,0:T(8,128)(2,1)S(1)}, bf16[4,128,128]{2,1,0:T(8,128)(2,1)S(1)}, u32[]{:S(2)}, u32[]{:S(2)}) collective-permute-start(bf16[4,128,128]{2,1,0:T(8,128)(2,1)S(1)} %get-tuple-element.209), channel_id=1, source_target_pairs={{60,0},{0,4},{4,8},{8,12},{12,16},{16,20},{20,24},{24,28},{28,32},... | collective-permute-start | bytes 393224 | tf_op jit(solution)/shard_map/while/body/eval_jaxpr/ppermute | solution.py:10
  107.3 12.9 %collective-permute-start = (bf16[4,128,128]{2,1,0:T(8,128)(2,1)S(1)}, bf16[4,128,128]{2,1,0:T(8,128)(2,1)S(1)}, u32[]{:S(2)}, u32[]{:S(2)}) collective-permute-start(bf16[4,128,128]{2,1,0:T(8,128)(2,1)S(1)} %get-tuple-element.209), channel_id=1, source_target_pairs={{60,0},{0,4},{4,8},{8,12},{12,16},{16,20},{20,24},{24,28},{28,32},... | collective-permute-start | bytes 393224 | tf_op jit(solution)/shard_map/while/body/eval_jaxpr/ppermute | solution.py:10
  125.3 12.9 %collective-permute-start = (bf16[4,128,128]{2,1,0:T(8,128)(2,1)S(1)}, bf16[4,128,128]{2,1,0:T(8,128)(2,1)S(1)}, u32[]{:S(2)}, u32[]{:S(2)}) collective-permute-start(bf16[4,128,128]{2,1,0:T(8,128)(2,1)S(1)} %get-tuple-element.209), channel_id=1, source_target_pairs={{60,0},{0,4},{4,8},{8,12},{12,16},{16,20},{20,24},{24,28},{28,32},... | collective-permute-start | bytes 393224 | tf_op jit(solution)/shard_map/while/body/eval_jaxpr/ppermute | solution.py:10
  143.4 12.9 %collective-permute-start = (bf16[4,128,128]{2,1,0:T(8,128)(2,1)S(1)}, bf16[4,128,128]{2,1,0:T(8,128)(2,1)S(1)}, u32[]{:S(2)}, u32[]{:S(2)}) collective-permute-start(bf16[4,128,128]{2,1,0:T(8,128)(2,1)S(1)} %get-tuple-element.209), channel_id=1, source_target_pairs={{60,0},{0,4},{4,8},{8,12},{12,16},{16,20},{20,24},{24,28},{28,32},... | collective-permute-start | bytes 393224 | tf_op jit(solution)/shard_map/while/body/eval_jaxpr/ppermute | solution.py:10
  161.4 12.9 %collective-permute-start = (bf16[4,128,128]{2,1,0:T(8,128)(2,1)S(1)}, bf16[4,128,128]{2,1,0:T(8,128)(2,1)S(1)}, u32[]{:S(2)}, u32[]{:S(2)}) collective-permute-start(bf16[4,128,128]{2,1,0:T(8,128)(2,1)S(1)} %get-tuple-element.209), channel_id=1, source_target_pairs={{60,0},{0,4},{4,8},{8,12},{12,16},{16,20},{20,24},{24,28},{28,32},... | collective-permute-start | bytes 393224 | tf_op jit(solution)/shard_map/while/body/eval_jaxpr/ppermute | solution.py:10
  179.4 12.9 %collective-permute-start = (bf16[4,128,128]{2,1,0:T(8,128)(2,1)S(1)}, bf16[4,128,128]{2,1,0:T(8,128)(2,1)S(1)}, u32[]{:S(2)}, u32[]{:S(2)}) collective-permute-start(bf16[4,128,128]{2,1,0:T(8,128)(2,1)S(1)} %get-tuple-element.209), channel_id=1, source_target_pairs={{60,0},{0,4},{4,8},{8,12},{12,16},{16,20},{20,24},{24,28},{28,32},... | collective-permute-start | bytes 393224 | tf_op jit(solution)/shard_map/while/body/eval_jaxpr/ppermute | solution.py:10
  197.4 12.9 %collective-permute-start = (bf16[4,128,128]{2,1,0:T(8,128)(2,1)S(1)}, bf16[4,128,128]{2,1,0:T(8,128)(2,1)S(1)}, u32[]{:S(2)}, u32[]{:S(2)}) collective-permute-start(bf16[4,128,128]{2,1,0:T(8,128)(2,1)S(1)} %get-tuple-element.209), channel_id=1, source_target_pairs={{60,0},{0,4},{4,8},{8,12},{12,16},{16,20},{20,24},{24,28},{28,32},... | collective-permute-start | bytes 393224 | tf_op jit(solution)/shard_map/while/body/eval_jaxpr/ppermute | solution.py:10
  215.5 12.9 %collective-permute-start = (bf16[4,128,128]{2,1,0:T(8,128)(2,1)S(1)}, bf16[4,128,128]{2,1,0:T(8,128)(2,1)S(1)}, u32[]{:S(2)}, u32[]{:S(2)}) collective-permute-start(bf16[4,128,128]{2,1,0:T(8,128)(2,1)S(1)} %get-tuple-element.209), channel_id=1, source_target_pairs={{60,0},{0,4},{4,8},{8,12},{12,16},{16,20},{20,24},{24,28},{28,32},... | collective-permute-start | bytes 393224 | tf_op jit(solution)/shard_map/while/body/eval_jaxpr/ppermute | solution.py:10
  233.5 12.9 %collective-permute-start = (bf16[4,128,128]{2,1,0:T(8,128)(2,1)S(1)}, bf16[4,128,128]{2,1,0:T(8,128)(2,1)S(1)}, u32[]{:S(2)}, u32[]{:S(2)}) collective-permute-start(bf16[4,128,128]{2,1,0:T(8,128)(2,1)S(1)} %get-tuple-element.209), channel_id=1, source_target_pairs={{60,0},{0,4},{4,8},{8,12},{12,16},{16,20},{20,24},{24,28},{28,32},... | collective-permute-start | bytes 393224 | tf_op jit(solution)/shard_map/while/body/eval_jaxpr/ppermute | solution.py:10
  251.5 12.9 %collective-permute-start = (bf16[4,128,128]{2,1,0:T(8,128)(2,1)S(1)}, bf16[4,128,128]{2,1,0:T(8,128)(2,1)S(1)}, u32[]{:S(2)}, u32[]{:S(2)}) collective-permute-start(bf16[4,128,128]{2,1,0:T(8,128)(2,1)S(1)} %get-tuple-element.209), channel_id=1, source_target_pairs={{60,0},{0,4},{4,8},{8,12},{12,16},{16,20},{20,24},{24,28},{28,32},... | collective-permute-start | bytes 393224 | tf_op jit(solution)/shard_map/while/body/eval_jaxpr/ppermute | solution.py:10
  269.5 12.9 %collective-permute-start = (bf16[4,128,128]{2,1,0:T(8,128)(2,1)S(1)}, bf16[4,128,128]{2,1,0:T(8,128)(2,1)S(1)}, u32[]{:S(2)}, u32[]{:S(2)}) collective-permute-start(bf16[4,128,128]{2,1,0:T(8,128)(2,1)S(1)} %get-tuple-element.209), channel_id=1, source_target_pairs={{60,0},{0,4},{4,8},{8,12},{12,16},{16,20},{20,24},{24,28},{28,32},... | collective-permute-start | bytes 393224 | tf_op jit(solution)/shard_map/while/body/eval_jaxpr/ppermute | solution.py:10
  287.6 12.9 %collective-permute-start = (bf16[4,128,128]{2,1,0:T(8,128)(2,1)S(1)}, bf16[4,128,128]{2,1,0:T(8,128)(2,1)S(1)}, u32[]{:S(2)}, u32[]{:S(2)}) collective-permute-start(bf16[4,128,128]{2,1,0:T(8,128)(2,1)S(1)} %get-tuple-element.209), channel_id=1, source_target_pairs={{60,0},{0,4},{4,8},{8,12},{12,16},{16,20},{20,24},{24,28},{28,32},... | collective-permute-start | bytes 393224 | tf_op jit(solution)/shard_map/while/body/eval_jaxpr/ppermute | solution.py:10
  305.6 12.9 %collective-permute-start = (bf16[4,128,128]{2,1,0:T(8,128)(2,1)S(1)}, bf16[4,128,128]{2,1,0:T(8,128)(2,1)S(1)}, u32[]{:S(2)}, u32[]{:S(2)}) collective-permute-start(bf16[4,128,128]{2,1,0:T(8,128)(2,1)S(1)} %get-tuple-element.209), channel_id=1, source_target_pairs={{60,0},{0,4},{4,8},{8,12},{12,16},{16,20},{20,24},{24,28},{28,32},... | collective-permute-start | bytes 393224 | tf_op jit(solution)/shard_map/while/body/eval_jaxpr/ppermute | solution.py:10
  323.6 12.9 %collective-permute-start = (bf16[4,128,128]{2,1,0:T(8,128)(2,1)S(1)}, bf16[4,128,128]{2,1,0:T(8,128)(2,1)S(1)}, u32[]{:S(2)}, u32[]{:S(2)}) collective-permute-start(bf16[4,128,128]{2,1,0:T(8,128)(2,1)S(1)} %get-tuple-element.209), channel_id=1, source_target_pairs={{60,0},{0,4},{4,8},{8,12},{12,16},{16,20},{20,24},{24,28},{28,32},... | collective-permute-start | bytes 393224 | tf_op jit(solution)/shard_map/while/body/eval_jaxpr/ppermute | solution.py:10
Sparse Core Ops, SparseCore 0:
  341.8 21.2 reduce-scatter.1
